TPU v7x, 32 devices: a whole 2x2x4 slice. The times are simulated.
32 devices in a mesh: loss: 4 (over x, core), tower: 4 (over z), pipe: 2 (over y).
Axes of the slice: x: 2, y: 2, z: 4, core: 2. Of those that a mesh axis runs over, the one named last changes fastest.
Arguments:
- image_feats: bfloat16 [4, 2, 24, 1536], P('loss', 'pipe', None, 'tower'), may hold values from -6 to 6
- text_tokens: bfloat16 [4, 2, 24, 64, 1152], P('loss', 'pipe', None, None, 'tower'), may hold values from -6 to 6
- lengths: int32 [4, 2, 24], P('loss', 'pipe'), may hold values from 1 to 64, as said below
- w_image: bfloat16 [1536, 1536], P('tower'), may hold values from -0.15625 to 0.15625
- w_text: bfloat16 [1152, 1536], P('tower'), may hold values from -0.1875 to 0.1875
- logit_scale: float32 [1], replicated, may hold values from 24 to 48
- logit_bias: float32 [1], replicated, may hold values from -4 to -2
Outputs:
- image_grad: float32 [4, 2, 24, 1536], P('loss', 'pipe', 'tower')
- text_grad: float32 [4, 2, 24, 1536], P('loss', 'pipe', 'tower')
Inputs may be any that keep to these rules, and one draw needn't show every extreme that they name: `lengths`: in every group of 24 captions one caption has 64 tokens and one has a single token.
All inputs are finite; a program needn't handle non-finite values.
Results may differ from a plain program's by a relative error of at most 0.0036.
The roundings to bfloat16 on the way count: a program that leaves them out, or rounds other values in their place, can miss the bound.
Values may be sent and summed in bfloat16 or wider, within the bound.
A program may use at most 64 MiB of HBM per device.

v0:
```python
import jax
import jax.numpy as jnp
from jax import lax
from jax.sharding import PartitionSpec as P


def normalize(raw):
    return raw * lax.rsqrt(jnp.sum(raw * raw, axis=-1, keepdims=True) + 1e-06)


def pair_terms(image_unit, texts, image_ids, text_ids, scale, shift):
    scores = jnp.dot(image_unit, texts.T, preferred_element_type=jnp.float32)
    match = (image_ids[:, None] == text_ids[None, :]).astype(jnp.float32)
    return (jax.nn.sigmoid(scale * scores + shift) - match).astype(jnp.bfloat16)


def per_device(image_feats, text_tokens, lengths, w_image, w_text, logit_scale, logit_bias):
    group = image_feats.shape[2]
    emb = w_image.shape[1]
    images = image_feats.reshape(group, image_feats.shape[3])
    words = text_tokens.reshape(group, text_tokens.shape[3], text_tokens.shape[4])
    counts = lengths.reshape(group)
    places = lax.broadcasted_iota(jnp.int32, (group, words.shape[1]), 1)
    keep = (places < counts[:, None]).astype(jnp.bfloat16)
    summed = jnp.einsum("bl,bld->bd", keep, words, preferred_element_type=jnp.float32)
    pooled = (summed / counts.astype(jnp.float32)[:, None]).astype(jnp.bfloat16)
    image_raw = lax.psum(jnp.dot(images, w_image, preferred_element_type=jnp.float32), "tower")
    towers = lax.axis_size("tower")
    sub = group // towers
    text_raw = lax.psum_scatter(
        jnp.dot(pooled, w_text, preferred_element_type=jnp.float32),
        "tower",
        scatter_dimension=0,
        tiled=True,
    )
    image_unit = normalize(image_raw).astype(jnp.bfloat16)
    text_unit = normalize(text_raw).astype(jnp.bfloat16)
    scale = logit_scale[0]
    shift = logit_bias[0]
    loss_at = lax.axis_index("loss")
    pipe_at = lax.axis_index("pipe")
    tower_at = lax.axis_index("tower")
    pipes = lax.axis_size("pipe")
    image_ids = (loss_at * pipes + pipe_at) * group + lax.iota(jnp.int32, group)
    texts = lax.all_gather(text_unit, ("loss", "pipe"), axis=0, tiled=True)
    spots = lax.iota(jnp.int32, texts.shape[0])
    text_ids = spots // sub * group + tower_at * sub + spots % sub
    grads = pair_terms(image_unit, texts, image_ids, text_ids, scale, shift)
    image_term = scale * jnp.dot(grads, texts, preferred_element_type=jnp.float32)
    text_grad = lax.psum_scatter(
        scale
        * lax.dot_general(
            grads, image_unit, (((0,), (0,)), ((), ())), preferred_element_type=jnp.float32
        ),
        ("loss", "pipe"),
        scatter_dimension=0,
        tiled=True,
    )
    image_grad = lax.psum_scatter(image_term, "tower", scatter_dimension=0, tiled=True)
    return (image_grad.reshape(1, 1, sub, emb), text_grad.reshape(1, 1, sub, emb))


def solution(mesh):
    return jax.shard_map(
        per_device,
        mesh=mesh,
        in_specs=(
            P("loss", "pipe", None, "tower"),
            P("loss", "pipe", None, None, "tower"),
            P("loss", "pipe", None),
            P("tower", None),
            P("tower", None),
            P(),
            P(),
        ),
        out_specs=(P("loss", "pipe", "tower", None), P("loss", "pipe", "tower", None)),
        check_vma=False,
    )
```

profile of v0, /device:TPU:0, one launch (start us, length us, event | category | flops | bytes accessed | tf_op | source)
XLA Modules:
  0.0 115.3 jit_solution(13100694398209393492)
XLA Ops:
  7.2 0.0 copy-start
  7.2 0.0 all-reduce.8.cloned.1.call-start
  7.2 0.8 bitcast_convert_fusion
  8.0 0.7 fusion.20
  8.8 1.6 %fusion.3 = f32[24,1,288]{2,1,0:T(1,128)S(1)} fusion(bf16[1,1,24,64,288]{4,3,2,1,0:T(8,128)(2,1)} %param.8, pred[24,64,1]{1,0,2:T(8,128)(4,1)S(1)} %fusion.20), kind=kOutput, calls=%fused_computation.2 | convolution fusion | flops 884736 | bytes 913920 | tf_op jit(solution)/shard_map/bl,bld->bd/dot_general | solution.py:25
  10.3 0.3 fusion.15
  10.7 15.8 %fusion = f32[8,1536]{1,0:T(8,128)S(1)} fusion(f32[24,1536]{1,0:T(8,128)S(1)} %fusion.15), kind=kCustom, calls=%all-reduce-scatter | all-reduce-scatter fusion | flops 49153 | bytes 197120
  26.5 2.4 %collective-permute-start = (f32[6,1536]{1,0:T(8,128)S(1)}, f32[6,1536]{1,0:T(8,128)S(1)}, u32[]{:S(2)}, u32[]{:S(2)}) collective-permute-start(f32[6,1536]{1,0:T(8,128)S(1)} %slice), channel_id=1, source_target_pairs={{0,2},{2,4},{4,6},{1,3},{3,5},{5,7},{8,10},{10,12},{12,14},{9,11},... | collective-permute-start | bytes 110600
  28.9 0.9 fusion.17
  29.9 0.0 all-reduce.8.cloned.1.call-update
  31.2 0.6 dynamic-slice.8
  31.8 0.7 dynamic-slice.16
  33.8 0.1 concatenate
  34.0 0.1 multiply_reduce_fusion.1
  34.1 0.1 fusion.14
  34.2 16.5 %all-gather = bf16[8,6,1536]{2,1,0:T(8,128)(2,1)S(1)} all-gather(bf16[1,6,1536]{2,1,0:T(8,128)(2,1)S(1)} %fusion.14), channel_id=1, replica_groups=mesh['loss'=4,'tower'=4,'pipe'=2] {'loss','pipe'}, dimensions={0}, use_global_device_ids=true | all-gather | bytes 165888 | tf_op jit(solution)/shard_map/all_gather | solution.py:45
  50.7 0.1 reshape.64
  50.8 12.4 %all-reduce.8.cloned.1.call-done = f32[24,1536]{1,0:T(8,128)} async-done(((f32[24,1536]{1,0:T(8,128)}), f32[24,1536]{1,0:T(8,128)}) %all-reduce.8.cloned.1.call-update) | async-done | bytes 147472 | tf_op jit(solution)/shard_map/psum | solution.py:27
  63.2 1.0 multiply_reduce_fusion
  64.3 1.2 fusion.11
  65.4 0.1 convolution_multiply_fusion.1
  65.6 14.5 %fusion.1 = f32[8,1536]{1,0:T(8,128)S(1)} fusion(f32[24,1536]{1,0:T(8,128)S(1)} %convolution_multiply_fusion.1), kind=kCustom, calls=%all-reduce-scatter.1 | all-reduce-scatter fusion | flops 49153 | bytes 197120
  80.0 1.8 %collective-permute-start.1 = (f32[6,1536]{1,0:T(8,128)S(1)}, f32[6,1536]{1,0:T(8,128)S(1)}, u32[]{:S(2)}, u32[]{:S(2)}) collective-permute-start(f32[6,1536]{1,0:T(8,128)S(1)} %slice.1), channel_id=1, source_target_pairs={{0,2},{2,4},{4,6},{1,3},{3,5},{5,7},{8,10},{10,12},{12,14},{9,11},... | collective-permute-start | bytes 110600
  81.9 1.2 convolution_multiply_fusion
  83.0 18.3 %fusion.2 = f32[8,1536]{1,0:T(8,128)S(1)} fusion(f32[48,1536]{1,0:T(8,128)S(1)} %convolution_multiply_fusion), kind=kCustom, calls=%all-reduce-scatter.2 | all-reduce-scatter fusion | flops 98305 | bytes 344576
  101.4 3.9 %collective-permute-start.2 = (f32[8,1536]{1,0:T(8,128)S(1)}, f32[8,1536]{1,0:T(8,128)S(1)}, u32[]{:S(2)}, u32[]{:S(2)}) collective-permute-start(f32[8,1536]{1,0:T(8,128)S(1)} %fusion.2), channel_id=1, source_target_pairs={{0,1},{1,8},{8,9},{9,16},{16,17},{17,24},{24,25},{2,3},{3,10},{10,... | collective-permute-start | bytes 147464
  105.3 1.3 %collective-permute-start.3 = (f32[6,1536]{1,0:T(8,128)S(1)}, f32[6,1536]{1,0:T(8,128)S(1)}, u32[]{:S(2)}, u32[]{:S(2)}) collective-permute-start(f32[6,1536]{1,0:T(8,128)S(1)} %slice.2), channel_id=1, source_target_pairs={{0,8},{1,9},{8,16},{9,17},{16,24},{17,25},{2,10},{3,11},{10,18},{1... | collective-permute-start | bytes 110600
  106.6 0.1 concatenate.1
  106.8 0.7 copy.13
  107.4 0.0 collective-permute-done.3
  107.5 0.2 concatenate.2
  107.8 0.7 copy.14
  (21 shorter events, 0.1 us)
Async XLA Ops:
  7.2 21.8 %copy-start = (bf16[384,1536]{1,0:T(8,128)(2,1)S(1)}, bf16[384,1536]{1,0:T(8,128)(2,1)}, u32[]{:S(2)}) copy-start(bf16[384,1536]{1,0:T(8,128)(2,1)} %param.10) | copy-start | bytes 3538948
  7.2 3.2 %copy-start.1 = (bf16[288,1536]{1,0:T(8,128)(2,1)S(1)}, bf16[288,1536]{1,0:T(8,128)(2,1)}, u32[]{:S(2)}) copy-start(bf16[288,1536]{1,0:T(8,128)(2,1)} %param.11) | copy-start | bytes 2654212
  7.2 56.0 %all-reduce.8.cloned.1.call-start = ((), (), s32[]{:S(2)}) async-start(), calls=%async_computation | async-start | bytes 294912 | tf_op jit(solution)/shard_map/psum | solution.py:27
  8.8 20.2 %copy-start.2 = (bf16[1,1,24,384]{3,2,1,0:T(8,128)(2,1)S(1)}, bf16[1,1,24,384]{3,2,1,0:T(8,128)(2,1)}, u32[]{:S(2)}) copy-start(bf16[1,1,24,384]{3,2,1,0:T(8,128)(2,1)} %param.7) | copy-start | bytes 55300
  10.6 20.6 %copy-start.4 = (u32[32]{0:T(128)S(1)}, u32[32]{0:T(128)}, u32[]{:S(2)}) copy-start(u32[32]{0:T(128)} %constant.48) | copy-start | bytes 388
  10.6 21.2 %copy-start.3 = (u32[32]{0:T(128)S(1)}, u32[32]{0:T(128)}, u32[]{:S(2)}) copy-start(u32[32]{0:T(128)} %constant.56) | copy-start | bytes 388
  26.5 7.4 %collective-permute-start = (f32[6,1536]{1,0:T(8,128)S(1)}, f32[6,1536]{1,0:T(8,128)S(1)}, u32[]{:S(2)}, u32[]{:S(2)}) collective-permute-start(f32[6,1536]{1,0:T(8,128)S(1)} %slice), channel_id=1, source_target_pairs={{0,2},{2,4},{4,6},{1,3},{3,5},{5,7},{8,10},{10,12},{12,14},{9,11},... | collective-permute-start | bytes 110600
  80.0 26.6 %collective-permute-start.1 = (f32[6,1536]{1,0:T(8,128)S(1)}, f32[6,1536]{1,0:T(8,128)S(1)}, u32[]{:S(2)}, u32[]{:S(2)}) collective-permute-start(f32[6,1536]{1,0:T(8,128)S(1)} %slice.1), channel_id=1, source_target_pairs={{0,2},{2,4},{4,6},{1,3},{3,5},{5,7},{8,10},{10,12},{12,14},{9,11},... | collective-permute-start | bytes 110600
  101.4 6.1 %collective-permute-start.2 = (f32[8,1536]{1,0:T(8,128)S(1)}, f32[8,1536]{1,0:T(8,128)S(1)}, u32[]{:S(2)}, u32[]{:S(2)}) collective-permute-start(f32[8,1536]{1,0:T(8,128)S(1)} %fusion.2), channel_id=1, source_target_pairs={{0,1},{1,8},{8,9},{9,16},{16,17},{17,24},{24,25},{2,3},{3,10},{10,... | collective-permute-start | bytes 147464
  105.3 2.2 %collective-permute-start.3 = (f32[6,1536]{1,0:T(8,128)S(1)}, f32[6,1536]{1,0:T(8,128)S(1)}, u32[]{:S(2)}, u32[]{:S(2)}) collective-permute-start(f32[6,1536]{1,0:T(8,128)S(1)} %slice.2), channel_id=1, source_target_pairs={{0,8},{1,9},{8,16},{9,17},{16,24},{17,25},{2,10},{3,11},{10,18},{1... | collective-permute-start | bytes 110600
Sparse Core Ops, SparseCore 0:
  30.0 33.1 all-reduce.7
where the time goes:
time: 117 us; the launch traced here: 115 us
  blocking collectives  65.1 us (56%)
  between operations  16.9 us (14%)
  waiting for transfers between devices  12.5 us (11%)
  starting transfers between devices  9.54 us (8%)
  matrix products  5.25 us (4%)
  local copies, waits for them, and re-layouts  3.18 us (3%)
  other arithmetic  2.8 us (2%)
    unnamed x3, blocking collectives  48.6 us
    all_gather x1, blocking collectives, per_device(): texts = lax.all_gather(text_unit, ('loss', 'pipe'), axis=0, tiled=True)  16.5 us
    psum x1, waiting for transfers between devices, per_device(): lax.psum(jnp.dot(images, w_image, preferred_element_type=jnp.float32), 't...  12.4 us
    unnamed x4, starting transfers between devices  9.5 us
    unnamed x21, local copies, waits for them, and re-layouts  3.15 us
  transfers between devices with their start and end apart: 5, of which 1 were waited for; matrix products, arithmetic and copies ran while one was open for 20% of the time, Pallas kernels for 0%

commit v1 on v0

v1 whole, which is shorter than its diff:
```python
import functools

import jax
import jax.numpy as jnp
from jax import lax
from jax.experimental import pallas as pl
from jax.experimental.pallas import tpu as pltpu
from jax.sharding import PartitionSpec as P

MESH = pl.DeviceIdType.MESH
WIRE = jnp.bfloat16
SUM = jnp.float32
F32 = jnp.float32
UNROLL = 16


def each(lo, hi, body):
    if hi - lo <= UNROLL:
        for k in range(lo, hi):
            body(k)
    else:
        lax.fori_loop(lo, hi, lambda k, c: (body(k), c)[1], 0)


def kernel(
    sub, towers, pipes, planes,
    scale_ref, shift_ref, feats_hbm, words_hbm, lens_hbm, wi_hbm, wt_hbm,
    image_out, text_out,
    feats, words, lens, wi, wt,
    part_i, part_t, got_i, got_t, images, texts, term_i, term_t, back_i, back_t,
    load_sem, s1, r1, s2, r2, s3, r3, s4, r4, s5, r5, s6, r6,
):
    pad = images.shape[1]
    group, width = feats.shape
    length = words.shape[1]
    emb = wi.shape[1]
    rows = towers * pad
    tower = lax.axis_index("tower")
    plane = lax.axis_index("loss") * pipes + lax.axis_index("pipe")

    def tower_peer(k):
        return {"tower": lax.rem(tower + k, towers)}

    def plane_peer(k):
        q = lax.rem(plane + k, planes)
        return {"loss": q // pipes, "pipe": lax.rem(q, pipes)}

    loads = []
    for n, (src, dst) in enumerate((
        (lens_hbm.at[0], lens),
        (words_hbm.at[0, 0], words),
        (wt_hbm, wt),
        (feats_hbm.at[0, 0], feats),
        (wi_hbm, wi),
    )):
        loads.append(pltpu.make_async_copy(src, dst, load_sem.at[n]))
        loads[-1].start()

    barrier = pltpu.get_barrier_semaphore()
    each(1, towers, lambda k: pl.semaphore_signal(
        barrier, inc=1, device_id=tower_peer(k), device_id_type=MESH))
    each(1, planes, lambda k: pl.semaphore_signal(
        barrier, inc=1, device_id=plane_peer(k), device_id_type=MESH))

    def source_row(shape):
        at = lax.broadcasted_iota(jnp.int32, shape, 0)
        r = at % pad
        return jnp.where(r < sub, at // pad * sub + r, -1)

    pick = (source_row((rows, group)) == lax.broadcasted_iota(jnp.int32, (rows, group), 1))

    def scatter(k, part, got, send, recv):
        return pltpu.make_async_remote_copy(
            src_ref=part.at[lax.rem(tower + k, towers)], dst_ref=got.at[k - 1],
            send_sem=send.at[k - 1], recv_sem=recv.at[k - 1],
            device_id=tower_peer(k), device_id_type=MESH)

    loads[0].wait()
    counts = jnp.sum(jnp.where(pick, lens[...].astype(F32), 0.0), axis=1, keepdims=True)
    spot = lax.broadcasted_iota(jnp.int32, (rows, group * length), 1)
    first = source_row((rows, group * length)) * length
    keep = (spot >= first) & (spot < first + counts.astype(jnp.int32)) & (first >= 0)
    keep = jnp.where(keep, 1.0, 0.0).astype(jnp.bfloat16)
    loads[1].wait()
    summed = jnp.dot(keep, words[...].reshape(group * length, words.shape[2]),
                     preferred_element_type=F32)
    pooled = (summed / jnp.maximum(counts, 1.0)).astype(jnp.bfloat16)
    loads[2].wait()
    raw_t = jnp.dot(pooled, wt[...], preferred_element_type=F32).reshape(towers, pad, emb)
    part_t[...] = raw_t
    pl.semaphore_wait(barrier, towers + planes - 2)
    each(1, towers, lambda k: scatter(k, part_t, got_t, s1, r1).start())

    loads[3].wait()
    moved = jnp.dot(jnp.where(pick, 1.0, 0.0).astype(jnp.bfloat16), feats[...],
                    preferred_element_type=F32).astype(jnp.bfloat16)
    loads[4].wait()
    raw_i = jnp.dot(moved, wi[...], preferred_element_type=F32).reshape(towers, pad, emb)
    part_i[...] = raw_i
    each(1, towers, lambda k: scatter(k, part_i, got_i, s2, r2).start())

    def unit(part, got, send, recv):
        each(1, towers, lambda k: scatter(k, part, got, send, recv).wait_recv())
        raw = part[tower]
        for k in range(towers - 1):
            raw = raw + got[k]
        size = jnp.sum(raw * raw, axis=-1, keepdims=True) + 1e-06
        return (raw * lax.rsqrt(size)).astype(jnp.bfloat16)

    def spread_t(k):
        return pltpu.make_async_remote_copy(
            src_ref=texts.at[plane], dst_ref=texts.at[plane],
            send_sem=s3.at[k - 1], recv_sem=r3.at[k - 1],
            device_id=plane_peer(k), device_id_type=MESH)

    def spread_i(k):
        return pltpu.make_async_remote_copy(
            src_ref=images.at[tower], dst_ref=images.at[tower],
            send_sem=s4.at[k - 1], recv_sem=r4.at[k - 1],
            device_id=tower_peer(k), device_id_type=MESH)

    texts[plane] = unit(part_t, got_t, s1, r1)
    each(1, planes, lambda k: spread_t(k).start())
    images[tower] = unit(part_i, got_i, s2, r2)
    each(1, towers, lambda k: spread_i(k).start())
    each(1, planes, lambda k: spread_t(k).wait_recv())
    each(1, towers, lambda k: spread_i(k).wait_recv())

    scale = scale_ref[0]
    shift = shift_ref[0]
    cols = planes * pad
    all_i = images[...].astype(F32).reshape(rows, emb).astype(jnp.bfloat16)
    all_t = texts[...].astype(F32).reshape(cols, emb).astype(jnp.bfloat16)
    scores = lax.dot_general(all_i, all_t, (((1,), (1,)), ((), ())), preferred_element_type=F32)
    at_i = lax.broadcasted_iota(jnp.int32, (rows, cols), 0) - tower * pad
    at_t = lax.broadcasted_iota(jnp.int32, (rows, cols), 1) - plane * pad
    match = jnp.where((at_i == at_t) & (at_i >= 0) & (at_i < pad), 1.0, 0.0)
    grads = jax.nn.sigmoid(scale * scores + shift) - match

    def back_image(k):
        return pltpu.make_async_remote_copy(
            src_ref=term_i.at[lax.rem(tower + k, towers)], dst_ref=back_i.at[k - 1],
            send_sem=s5.at[k - 1], recv_sem=r5.at[k - 1],
            device_id=tower_peer(k), device_id_type=MESH)

    def back_text(k):
        return pltpu.make_async_remote_copy(
            src_ref=term_t.at[lax.rem(plane + k, planes)], dst_ref=back_t.at[k - 1],
            send_sem=s6.at[k - 1], recv_sem=r6.at[k - 1],
            device_id=plane_peer(k), device_id_type=MESH)

    grads_t = grads.T.astype(jnp.bfloat16)
    sums_t = jnp.dot(grads_t, all_i, preferred_element_type=F32)
    term_t[...] = sums_t.reshape(planes, pad, emb).astype(WIRE)
    each(1, planes, lambda k: back_text(k).start())
    sums_i = jnp.dot(grads.astype(jnp.bfloat16), all_t, preferred_element_type=F32)
    term_i[...] = sums_i.reshape(towers, pad, emb).astype(WIRE)
    each(1, towers, lambda k: back_image(k).start())

    mine_t = lax.broadcasted_iota(jnp.int32, (pad, cols), 0) + plane * pad
    mine_t = jnp.where(mine_t == lax.broadcasted_iota(jnp.int32, (pad, cols), 1), 1.0, 0.0)
    mine_i = lax.broadcasted_iota(jnp.int32, (pad, rows), 0) + tower * pad
    mine_i = jnp.where(mine_i == lax.broadcasted_iota(jnp.int32, (pad, rows), 1), 1.0, 0.0)
    own_gt = jnp.dot(mine_t.astype(jnp.bfloat16), grads_t, preferred_element_type=F32)
    own_gi = jnp.dot(mine_i.astype(jnp.bfloat16), grads.astype(jnp.bfloat16),
                     preferred_element_type=F32)
    own_t = jnp.dot(own_gt.astype(jnp.bfloat16), all_i, preferred_element_type=F32)
    own_i = jnp.dot(own_gi.astype(jnp.bfloat16), all_t, preferred_element_type=F32)

    each(1, planes, lambda k: back_text(k).wait_recv())
    text_out[0, 0] = (scale * (own_t + jnp.sum(back_t[...].astype(F32), axis=0)))[:sub]
    each(1, towers, lambda k: back_image(k).wait_recv())
    image_out[0, 0] = (scale * (own_i + jnp.sum(back_i[...].astype(F32), axis=0)))[:sub]

    each(1, towers, lambda k: scatter(k, part_t, got_t, s1, r1).wait_send())
    each(1, towers, lambda k: scatter(k, part_i, got_i, s2, r2).wait_send())
    each(1, planes, lambda k: spread_t(k).wait_send())
    each(1, towers, lambda k: spread_i(k).wait_send())
    each(1, towers, lambda k: back_image(k).wait_send())
    each(1, planes, lambda k: back_text(k).wait_send())


def per_device(towers, pipes, planes, image_feats, text_tokens, lengths, w_image, w_text,
               logit_scale, logit_bias):
    group = image_feats.shape[2]
    emb = w_image.shape[1]
    sub = group // towers
    pad = -(-sub // 8) * 8
    out = jax.ShapeDtypeStruct((1, 1, sub, emb), F32)
    sems = []
    for n in (towers, towers, planes, towers, towers, planes):
        sems += [pltpu.SemaphoreType.DMA((n - 1,))] * 2
    return pl.pallas_call(
        functools.partial(kernel, sub, towers, pipes, planes),
        out_shape=(out, out),
        in_specs=[pl.BlockSpec(memory_space=pltpu.SMEM)] * 2
        + [pl.BlockSpec(memory_space=pl.ANY)] * 5,
        out_specs=(pl.BlockSpec(memory_space=pltpu.VMEM),) * 2,
        scratch_shapes=[
            pltpu.VMEM(image_feats.shape[2:], image_feats.dtype),
            pltpu.VMEM(text_tokens.shape[2:], text_tokens.dtype),
            pltpu.VMEM(lengths.shape[1:], lengths.dtype),
            pltpu.VMEM(w_image.shape, w_image.dtype),
            pltpu.VMEM(w_text.shape, w_text.dtype),
            pltpu.VMEM((towers, pad, emb), SUM),
            pltpu.VMEM((towers, pad, emb), SUM),
            pltpu.VMEM((towers - 1, pad, emb), SUM),
            pltpu.VMEM((towers - 1, pad, emb), SUM),
            pltpu.VMEM((towers, pad, emb), jnp.bfloat16),
            pltpu.VMEM((planes, pad, emb), jnp.bfloat16),
            pltpu.VMEM((towers, pad, emb), WIRE),
            pltpu.VMEM((planes, pad, emb), WIRE),
            pltpu.VMEM((towers - 1, pad, emb), WIRE),
            pltpu.VMEM((planes - 1, pad, emb), WIRE),
            pltpu.SemaphoreType.DMA((5,)),
        ] + sems,
        compiler_params=pltpu.CompilerParams(collective_id=0, has_side_effects=True),
    )(logit_scale, logit_bias, image_feats, text_tokens, lengths, w_image, w_text)


def solution(mesh):
    shape = dict(mesh.shape)
    planes = shape["loss"] * shape["pipe"]
    return jax.shard_map(
        functools.partial(per_device, shape["tower"], shape["pipe"], planes),
        mesh=mesh,
        in_specs=(
            P("loss", "pipe", None, "tower"),
            P("loss", "pipe", None, None, "tower"),
            P("loss", "pipe", None),
            P("tower", None),
            P("tower", None),
            P(),
            P(),
        ),
        out_specs=(P("loss", "pipe", "tower", None), P("loss", "pipe", "tower", None)),
        check_vma=False,
    )
```

time: 117 us -> 30.6 us (0.26); the launches traced: 115 us -> 30.3 us
  blocking collectives: 65.1 us -> 0 us
  Pallas kernels: 0 us -> 25.5 us
  between operations: 16.9 us -> 1.93 us
  waiting for transfers between devices: 12.5 us -> 0 us
  starting transfers between devices: 9.54 us -> 0 us
  matrix products: 5.25 us -> 0 us
  other arithmetic: 2.8 us -> 0 us
    unnamed x3 -> x0, blocking collectives: 48.6 us -> none
    pallas_call x0 -> x1, Pallas kernels: none -> 25.5 us  [per_device(): pl.pallas_call(functools.partial(kernel, sub, towers, pipes, planes), out...]
    all_gather x1 -> x0, blocking collectives: 16.5 us -> none  [per_device(): texts = lax.all_gather(text_unit, ('loss', 'pipe'), axis=0, tiled=True)]
    psum x1 -> x0, waiting for transfers between devices: 12.4 us -> none  [per_device(): lax.psum(jnp.dot(images, w_image, preferred_element_type=jnp.float32), 't...]
    unnamed x4 -> x0, starting transfers between devices: 9.5 us -> none
    dot_general x6 -> x0, matrix products: 5.25 us -> none  [the longest x1 1.59 us: per_device(): jnp.einsum('bl,bld->bd', keep, words, preferred_element_type=jnp.float32)]
    unnamed x21 -> x0, local copies, waits for them, and re-layouts: 3.15 us -> none
    pallas_call x0 -> x2, local copies, waits for them, and re-layouts: none -> 2.9 us  [per_device(): pl.pallas_call(functools.partial(kernel, sub, towers, pipes, planes), out...]
  transfers between devices with their start and end apart: 5 -> 0, of which waited for: 1 -> 0; matrix products, arithmetic and copies ran while one was open for 20% -> 0% of each run, Pallas kernels for 0% -> 0%
where the time goes in v1:
time: 30.6 us; the launch traced here: 30.3 us
  Pallas kernels  25.5 us (83%)
  local copies, waits for them, and re-layouts  2.9 us (9%)
  between operations  1.93 us (6%)
    pallas_call x1, Pallas kernels, per_device(): pl.pallas_call(functools.partial(kernel, sub, towers, pipes, planes), out...  25.5 us
    pallas_call x2, local copies, waits for them, and re-layouts, per_device(): pl.pallas_call(functools.partial(kernel, sub, towers, pipes, planes), out...  2.9 us

profile of v1, /device:TPU:0, one launch (start us, length us, event | category | flops | bytes accessed | tf_op | source)
XLA Modules:
  0.0 30.3 jit_solution(12407569774789981922)
XLA Ops:
  1.9 25.5 %shard_map.86 = (f32[1,1,6,1536]{3,2,1,0:T(8,128)}, f32[1,1,6,1536]{3,2,1,0:T(8,128)}) custom-call(f32[1]{0:T(128)S(6)} %copy.11.scale_ref, f32[1]{0:T(128)S(6)} %copy.12.shift_ref, bf16[1,1,24,384]{3,2,1,0:T(8,128)(2,1)} %feats_hbm.1, bf16[1,1,24,64,288]{4,3,2,1,0:T(8,128)(2,1)} %words_hbm.1, s32[1,1,24]{2,1,0:T(1,128)} %lens_hbm.1, ...), custom_call_target="tpu_custom_call" | custom-call | tf_op jit(solution)/shard_map/pallas_call | solution.py:193
  27.4 1.5 %copy.9 = f32[1,1,6,1536]{3,1,2,0:T(1,128)} copy(f32[1,1,6,1536]{3,2,1,0:T(8,128)} %get-tuple-element.2) | data formatting | bytes 73728 | tf_op jit(solution)/shard_map/pallas_call | solution.py:193
  28.9 1.5 %copy.10 = f32[1,1,6,1536]{3,1,2,0:T(1,128)} copy(f32[1,1,6,1536]{3,2,1,0:T(8,128)} %get-tuple-element.3) | data formatting | bytes 73728 | tf_op jit(solution)/shard_map/pallas_call | solution.py:193

commit v2 on v1

--- a/solution.py
+++ b/solution.py
@@ -24,9 +24,9 @@
 
 def kernel(
     sub, towers, pipes, planes,
-    scale_ref, shift_ref, feats_hbm, words_hbm, lens_hbm, wi_hbm, wt_hbm,
+    scale_hbm, shift_hbm, feats_hbm, words_hbm, lens_hbm, wi_hbm, wt_hbm,
     image_out, text_out,
-    feats, words, lens, wi, wt,
+    scale_ref, shift_ref, feats, words, lens, wi, wt,
     part_i, part_t, got_i, got_t, images, texts, term_i, term_t, back_i, back_t,
     load_sem, s1, r1, s2, r2, s3, r3, s4, r4, s5, r5, s6, r6,
 ):
@@ -52,6 +52,8 @@
         (wt_hbm, wt),
         (feats_hbm.at[0, 0], feats),
         (wi_hbm, wi),
+        (scale_hbm, scale_ref),
+        (shift_hbm, shift_ref),
     )):
         loads.append(pltpu.make_async_copy(src, dst, load_sem.at[n]))
         loads[-1].start()
@@ -126,6 +128,8 @@
     each(1, planes, lambda k: spread_t(k).wait_recv())
     each(1, towers, lambda k: spread_i(k).wait_recv())
 
+    loads[5].wait()
+    loads[6].wait()
     scale = scale_ref[0]
     shift = shift_ref[0]
     cols = planes * pad
@@ -168,9 +172,9 @@
     own_i = jnp.dot(own_gi.astype(jnp.bfloat16), all_t, preferred_element_type=F32)
 
     each(1, planes, lambda k: back_text(k).wait_recv())
-    text_out[0, 0] = (scale * (own_t + jnp.sum(back_t[...].astype(F32), axis=0)))[:sub]
+    text_out[:, 0, :] = (own_t + jnp.sum(back_t[...].astype(F32), axis=0))[:sub]
     each(1, towers, lambda k: back_image(k).wait_recv())
-    image_out[0, 0] = (scale * (own_i + jnp.sum(back_i[...].astype(F32), axis=0)))[:sub]
+    image_out[:, 0, :] = (own_i + jnp.sum(back_i[...].astype(F32), axis=0))[:sub]
 
     each(1, towers, lambda k: scatter(k, part_t, got_t, s1, r1).wait_send())
     each(1, towers, lambda k: scatter(k, part_i, got_i, s2, r2).wait_send())
@@ -180,23 +184,30 @@
     each(1, planes, lambda k: back_text(k).wait_send())
 
 
+def finish(scale_ref, image_ref, text_ref, image_out, text_out):
+    image_out[...] = scale_ref[0] * image_ref[...]
+    text_out[...] = scale_ref[0] * text_ref[...]
+
+
 def per_device(towers, pipes, planes, image_feats, text_tokens, lengths, w_image, w_text,
                logit_scale, logit_bias):
     group = image_feats.shape[2]
     emb = w_image.shape[1]
     sub = group // towers
-    pad = -(-sub // 8) * 8
-    out = jax.ShapeDtypeStruct((1, 1, sub, emb), F32)
+    pad = sub
+    out = jax.ShapeDtypeStruct((sub, 1, emb), F32)
     sems = []
     for n in (towers, towers, planes, towers, towers, planes):
         sems += [pltpu.SemaphoreType.DMA((n - 1,))] * 2
-    return pl.pallas_call(
+    outs = pl.pallas_call(
         functools.partial(kernel, sub, towers, pipes, planes),
         out_shape=(out, out),
-        in_specs=[pl.BlockSpec(memory_space=pltpu.SMEM)] * 2
+        in_specs=[pl.BlockSpec(memory_space=pltpu.HBM)] * 2
         + [pl.BlockSpec(memory_space=pl.ANY)] * 5,
         out_specs=(pl.BlockSpec(memory_space=pltpu.VMEM),) * 2,
         scratch_shapes=[
+            pltpu.SMEM(logit_scale.shape, F32),
+            pltpu.SMEM(logit_bias.shape, F32),
             pltpu.VMEM(image_feats.shape[2:], image_feats.dtype),
             pltpu.VMEM(text_tokens.shape[2:], text_tokens.dtype),
             pltpu.VMEM(lengths.shape[1:], lengths.dtype),
@@ -212,10 +223,18 @@
             pltpu.VMEM((planes, pad, emb), WIRE),
             pltpu.VMEM((towers - 1, pad, emb), WIRE),
             pltpu.VMEM((planes - 1, pad, emb), WIRE),
-            pltpu.SemaphoreType.DMA((5,)),
+            pltpu.SemaphoreType.DMA((7,)),
         ] + sems,
         compiler_params=pltpu.CompilerParams(collective_id=0, has_side_effects=True),
     )(logit_scale, logit_bias, image_feats, text_tokens, lengths, w_image, w_text)
+    outs = pl.pallas_call(
+        finish,
+        out_shape=(out, out),
+        in_specs=[pl.BlockSpec(memory_space=pltpu.SMEM)]
+        + [pl.BlockSpec(memory_space=pltpu.VMEM)] * 2,
+        out_specs=(pl.BlockSpec(memory_space=pltpu.VMEM),) * 2,
+    )(logit_scale, *outs)
+    return tuple(o.reshape(1, 1, sub, emb) for o in outs)
 
 
 def solution(mesh):

time: 30.6 us -> 29 us (0.948)
  local copies, waits for them, and re-layouts: 2.9 us -> 0 us
  Pallas kernels: 25.5 us -> 26.9 us
    pallas_call x2 -> x0, local copies, waits for them, and re-layouts: 2.9 us -> none  [per_device(): pl.pallas_call(functools.partial(kernel, sub, towers, pipes, planes), out...]
    pallas_call x0 -> x1, Pallas kernels: none -> 1.42 us  [per_device(): pl.pallas_call(finish, out_shape=(out, out), in_specs=[pl.BlockSpec(memor...]
where the time goes in v2:
time: 29 us; the launch traced here: 28.8 us
  Pallas kernels  26.9 us (93%)
  between operations  1.93 us (7%)
    pallas_call x1, Pallas kernels, per_device(): pl.pallas_call(functools.partial(kernel, sub, towers, pipes, planes), out...  25.5 us
    pallas_call x1, Pallas kernels, per_device(): pl.pallas_call(finish, out_shape=(out, out), in_specs=[pl.BlockSpec(memor...  1.42 us

profile of v2, /device:TPU:0, one launch (start us, length us, event | category | flops | bytes accessed | tf_op | source)
XLA Modules:
  0.0 28.8 jit_solution(8198589827676261529)
XLA Ops:
  1.9 25.5 %shard_map.86 = (f32[6,1,1536]{2,1,0:T(1,128)}, f32[6,1,1536]{2,1,0:T(1,128)}) custom-call(f32[1]{0:T(128)S(6)} %copy.11.scale_hbm.scale_ref, f32[1]{0:T(128)S(6)} %copy.12.shift_hbm, bf16[1,1,24,384]{3,2,1,0:T(8,128)(2,1)} %feats_hbm.1, bf16[1,1,24,64,288]{4,3,2,1,0:T(8,128)(2,1)} %words_hbm.1, s32[1,1,24]{2,1,0:T(1,128)} %lens_hbm.1, ...), custom_call_target="tpu_custom_call" | custom-call | tf_op jit(solution)/shard_map/pallas_call | solution.py:202
  27.4 1.4 %shard_map.87 = (f32[6,1,1536]{2,1,0:T(1,128)}, f32[6,1,1536]{2,1,0:T(1,128)}) custom-call(f32[1]{0:T(128)S(6)} %copy.11.scale_hbm.scale_ref, f32[6,1,1536]{2,1,0:T(1,128)} %get-tuple-element.6.image_ref, f32[6,1,1536]{2,1,0:T(1,128)} %get-tuple-element.7.text_ref), custom_call_target="tpu_custom_call" | custom-call | tf_op jit(solution)/shard_map/pallas_call | solution.py:230

commit v3 on v2

--- a/solution.py
+++ b/solution.py
@@ -12,6 +12,7 @@
 SUM = jnp.float32
 F32 = jnp.float32
 UNROLL = 16
+LANES = 128
 
 
 def each(lo, hi, body):
@@ -28,9 +29,9 @@
     image_out, text_out,
     scale_ref, shift_ref, feats, words, lens, wi, wt,
     part_i, part_t, got_i, got_t, images, texts, term_i, term_t, back_i, back_t,
-    load_sem, s1, r1, s2, r2, s3, r3, s4, r4, s5, r5, s6, r6,
+    flat, load_sem, s1, r1, s2, r2, s3, r3, s4, r4, s5, r5, s6, r6,
 ):
-    pad = images.shape[1]
+    pad = -(-sub // 8) * 8
     group, width = feats.shape
     length = words.shape[1]
     emb = wi.shape[1]
@@ -77,6 +78,12 @@
             send_sem=send.at[k - 1], recv_sem=recv.at[k - 1],
             device_id=tower_peer(k), device_id_type=MESH)
 
+    def pack(part, raw):
+        for d in range(towers):
+            for c in range(emb // LANES):
+                part[d, c * sub:(c + 1) * sub, :] = raw[
+                    d * pad:d * pad + sub, c * LANES:(c + 1) * LANES]
+
     loads[0].wait()
     counts = jnp.sum(jnp.where(pick, lens[...].astype(F32), 0.0), axis=1, keepdims=True)
     spot = lax.broadcasted_iota(jnp.int32, (rows, group * length), 1)
@@ -88,8 +95,8 @@
                      preferred_element_type=F32)
     pooled = (summed / jnp.maximum(counts, 1.0)).astype(jnp.bfloat16)
     loads[2].wait()
-    raw_t = jnp.dot(pooled, wt[...], preferred_element_type=F32).reshape(towers, pad, emb)
-    part_t[...] = raw_t
+    raw_t = jnp.dot(pooled, wt[...], preferred_element_type=F32)
+    pack(part_t, raw_t)
     pl.semaphore_wait(barrier, towers + planes - 2)
     each(1, towers, lambda k: scatter(k, part_t, got_t, s1, r1).start())
 
@@ -97,15 +104,24 @@
     moved = jnp.dot(jnp.where(pick, 1.0, 0.0).astype(jnp.bfloat16), feats[...],
                     preferred_element_type=F32).astype(jnp.bfloat16)
     loads[4].wait()
-    raw_i = jnp.dot(moved, wi[...], preferred_element_type=F32).reshape(towers, pad, emb)
-    part_i[...] = raw_i
+    raw_i = jnp.dot(moved, wi[...], preferred_element_type=F32)
+    pack(part_i, raw_i)
     each(1, towers, lambda k: scatter(k, part_i, got_i, s2, r2).start())
+
+    def padded(x):
+        x = x.astype(F32)
+        if pad > sub:
+            x = jnp.concatenate([x, jnp.zeros((x.shape[0], pad - sub, emb), F32)], axis=1)
+        return x.reshape(x.shape[0] * pad, emb).astype(jnp.bfloat16)
 
     def unit(part, got, send, recv):
         each(1, towers, lambda k: scatter(k, part, got, send, recv).wait_recv())
         raw = part[tower]
         for k in range(towers - 1):
             raw = raw + got[k]
+        flat[...] = raw
+        raw = jnp.concatenate(
+            [flat[c * sub:(c + 1) * sub, :] for c in range(emb // LANES)], axis=1)
         size = jnp.sum(raw * raw, axis=-1, keepdims=True) + 1e-06
         return (raw * lax.rsqrt(size)).astype(jnp.bfloat16)
 
@@ -133,8 +149,8 @@
     scale = scale_ref[0]
     shift = shift_ref[0]
     cols = planes * pad
-    all_i = images[...].astype(F32).reshape(rows, emb).astype(jnp.bfloat16)
-    all_t = texts[...].astype(F32).reshape(cols, emb).astype(jnp.bfloat16)
+    all_i = padded(images[...])
+    all_t = padded(texts[...])
     scores = lax.dot_general(all_i, all_t, (((1,), (1,)), ((), ())), preferred_element_type=F32)
     at_i = lax.broadcasted_iota(jnp.int32, (rows, cols), 0) - tower * pad
     at_t = lax.broadcasted_iota(jnp.int32, (rows, cols), 1) - plane * pad
@@ -155,10 +171,10 @@
 
     grads_t = grads.T.astype(jnp.bfloat16)
     sums_t = jnp.dot(grads_t, all_i, preferred_element_type=F32)
-    term_t[...] = sums_t.reshape(planes, pad, emb).astype(WIRE)
+    term_t[...] = sums_t.reshape(planes, pad, emb)[:, :sub].astype(WIRE)
     each(1, planes, lambda k: back_text(k).start())
     sums_i = jnp.dot(grads.astype(jnp.bfloat16), all_t, preferred_element_type=F32)
-    term_i[...] = sums_i.reshape(towers, pad, emb).astype(WIRE)
+    term_i[...] = sums_i.reshape(towers, pad, emb)[:, :sub].astype(WIRE)
     each(1, towers, lambda k: back_image(k).start())
 
     mine_t = lax.broadcasted_iota(jnp.int32, (pad, cols), 0) + plane * pad
@@ -172,9 +188,9 @@
     own_i = jnp.dot(own_gi.astype(jnp.bfloat16), all_t, preferred_element_type=F32)
 
     each(1, planes, lambda k: back_text(k).wait_recv())
-    text_out[:, 0, :] = (own_t + jnp.sum(back_t[...].astype(F32), axis=0))[:sub]
+    text_out[:, 0, :] = (own_t[:sub] + jnp.sum(back_t[...].astype(F32), axis=0))
     each(1, towers, lambda k: back_image(k).wait_recv())
-    image_out[:, 0, :] = (own_i + jnp.sum(back_i[...].astype(F32), axis=0))[:sub]
+    image_out[:, 0, :] = (own_i[:sub] + jnp.sum(back_i[...].astype(F32), axis=0))
 
     each(1, towers, lambda k: scatter(k, part_t, got_t, s1, r1).wait_send())
     each(1, towers, lambda k: scatter(k, part_i, got_i, s2, r2).wait_send())
@@ -194,7 +210,6 @@
     group = image_feats.shape[2]
     emb = w_image.shape[1]
     sub = group // towers
-    pad = sub
     out = jax.ShapeDtypeStruct((sub, 1, emb), F32)
     sems = []
     for n in (towers, towers, planes, towers, towers, planes):
@@ -213,16 +228,17 @@
             pltpu.VMEM(lengths.shape[1:], lengths.dtype),
             pltpu.VMEM(w_image.shape, w_image.dtype),
             pltpu.VMEM(w_text.shape, w_text.dtype),
-            pltpu.VMEM((towers, pad, emb), SUM),
-            pltpu.VMEM((towers, pad, emb), SUM),
-            pltpu.VMEM((towers - 1, pad, emb), SUM),
-            pltpu.VMEM((towers - 1, pad, emb), SUM),
-            pltpu.VMEM((towers, pad, emb), jnp.bfloat16),
-            pltpu.VMEM((planes, pad, emb), jnp.bfloat16),
-            pltpu.VMEM((towers, pad, emb), WIRE),
-            pltpu.VMEM((planes, pad, emb), WIRE),
-            pltpu.VMEM((towers - 1, pad, emb), WIRE),
-            pltpu.VMEM((planes - 1, pad, emb), WIRE),
+            pltpu.VMEM((towers, sub * emb // LANES, LANES), SUM),
+            pltpu.VMEM((towers, sub * emb // LANES, LANES), SUM),
+            pltpu.VMEM((towers - 1, sub * emb // LANES, LANES), SUM),
+            pltpu.VMEM((towers - 1, sub * emb // LANES, LANES), SUM),
+            pltpu.VMEM((towers, sub, emb), jnp.bfloat16),
+            pltpu.VMEM((planes, sub, emb), jnp.bfloat16),
+            pltpu.VMEM((towers, sub, emb), WIRE),
+            pltpu.VMEM((planes, sub, emb), WIRE),
+            pltpu.VMEM((towers - 1, sub, emb), WIRE),
+            pltpu.VMEM((planes - 1, sub, emb), WIRE),
+            pltpu.VMEM((sub * emb // LANES, LANES), SUM),
             pltpu.SemaphoreType.DMA((7,)),
         ] + sems,
         compiler_params=pltpu.CompilerParams(collective_id=0, has_side_effects=True),

time: 29 us -> 27.1 us (0.934)
  Pallas kernels: 26.9 us -> 24.9 us
    pallas_call x1, Pallas kernels: 25.5 us -> 23.5 us  [per_device(): pl.pallas_call(functools.partial(kernel, sub, towers, pipes, planes), out...]
where the time goes in v3:
time: 27.1 us; the launch traced here: 26.9 us
  Pallas kernels  24.9 us (92%)
  between operations  1.93 us (7%)
    pallas_call x1, Pallas kernels, per_device(): pl.pallas_call(functools.partial(kernel, sub, towers, pipes, planes), out...  23.5 us
    pallas_call x1, Pallas kernels, per_device(): pl.pallas_call(finish, out_shape=(out, out), in_specs=[pl.BlockSpec(memor...  1.42 us

profile of v3, /device:TPU:0, one launch (start us, length us, event | category | flops | bytes accessed | tf_op | source)
XLA Modules:
  0.0 26.9 jit_solution(9193090875014944252)
XLA Ops:
  1.9 23.5 %shard_map.86 = (f32[6,1,1536]{2,1,0:T(1,128)}, f32[6,1,1536]{2,1,0:T(1,128)}) custom-call(f32[1]{0:T(128)S(6)} %copy.11.scale_hbm.scale_ref, f32[1]{0:T(128)S(6)} %copy.12.shift_hbm, bf16[1,1,24,384]{3,2,1,0:T(8,128)(2,1)} %feats_hbm.1, bf16[1,1,24,64,288]{4,3,2,1,0:T(8,128)(2,1)} %words_hbm.1, s32[1,1,24]{2,1,0:T(1,128)} %lens_hbm.1, ...), custom_call_target="tpu_custom_call" | custom-call | tf_op jit(solution)/shard_map/pallas_call | solution.py:217
  25.4 1.4 %shard_map.87 = (f32[6,1,1536]{2,1,0:T(1,128)}, f32[6,1,1536]{2,1,0:T(1,128)}) custom-call(f32[1]{0:T(128)S(6)} %copy.11.scale_hbm.scale_ref, f32[6,1,1536]{2,1,0:T(1,128)} %get-tuple-element.6.image_ref, f32[6,1,1536]{2,1,0:T(1,128)} %get-tuple-element.7.text_ref), custom_call_target="tpu_custom_call" | custom-call | tf_op jit(solution)/shard_map/pallas_call | solution.py:246

commit v4 on v3

--- a/solution.py
+++ b/solution.py
@@ -169,13 +169,13 @@
             send_sem=s6.at[k - 1], recv_sem=r6.at[k - 1],
             device_id=plane_peer(k), device_id_type=MESH)
 
+    sums_i = jnp.dot(grads.astype(jnp.bfloat16), all_t, preferred_element_type=F32)
+    term_i[...] = sums_i.reshape(towers, pad, emb)[:, :sub].astype(WIRE)
+    each(1, towers, lambda k: back_image(k).start())
     grads_t = grads.T.astype(jnp.bfloat16)
     sums_t = jnp.dot(grads_t, all_i, preferred_element_type=F32)
     term_t[...] = sums_t.reshape(planes, pad, emb)[:, :sub].astype(WIRE)
     each(1, planes, lambda k: back_text(k).start())
-    sums_i = jnp.dot(grads.astype(jnp.bfloat16), all_t, preferred_element_type=F32)
-    term_i[...] = sums_i.reshape(towers, pad, emb)[:, :sub].astype(WIRE)
-    each(1, towers, lambda k: back_image(k).start())
 
     mine_t = lax.broadcasted_iota(jnp.int32, (pad, cols), 0) + plane * pad
     mine_t = jnp.where(mine_t == lax.broadcasted_iota(jnp.int32, (pad, cols), 1), 1.0, 0.0)

time: 27.1 us -> 26.9 us (level)
  no operation moved by 1% of the time
where the time goes in v4:
time: 26.9 us; the launch traced here: 26.7 us
  Pallas kernels  24.7 us (92%)
  between operations  1.93 us (7%)
    pallas_call x1, Pallas kernels, per_device(): pl.pallas_call(functools.partial(kernel, sub, towers, pipes, planes), out...  23.3 us
    pallas_call x1, Pallas kernels, per_device(): pl.pallas_call(finish, out_shape=(out, out), in_specs=[pl.BlockSpec(memor...  1.42 us

profile of v4, /device:TPU:0, one launch (start us, length us, event | category | flops | bytes accessed | tf_op | source)
XLA Modules:
  0.0 26.7 jit_solution(12218984499779832021)
XLA Ops:
  1.9 23.3 %shard_map.86 = (f32[6,1,1536]{2,1,0:T(1,128)}, f32[6,1,1536]{2,1,0:T(1,128)}) custom-call(f32[1]{0:T(128)S(6)} %copy.11.scale_hbm.scale_ref, f32[1]{0:T(128)S(6)} %copy.12.shift_hbm, bf16[1,1,24,384]{3,2,1,0:T(8,128)(2,1)} %feats_hbm.1, bf16[1,1,24,64,288]{4,3,2,1,0:T(8,128)(2,1)} %words_hbm.1, s32[1,1,24]{2,1,0:T(1,128)} %lens_hbm.1, ...), custom_call_target="tpu_custom_call" | custom-call | tf_op jit(solution)/shard_map/pallas_call | solution.py:217
  25.2 1.4 %shard_map.87 = (f32[6,1,1536]{2,1,0:T(1,128)}, f32[6,1,1536]{2,1,0:T(1,128)}) custom-call(f32[1]{0:T(128)S(6)} %copy.11.scale_hbm.scale_ref, f32[6,1,1536]{2,1,0:T(1,128)} %get-tuple-element.6.image_ref, f32[6,1,1536]{2,1,0:T(1,128)} %get-tuple-element.7.text_ref), custom_call_target="tpu_custom_call" | custom-call | tf_op jit(solution)/shard_map/pallas_call | solution.py:246
